TPU v7x, 32 devices: a whole 2x2x4 slice. The times are simulated.
32 devices in a mesh: term: 4 (over y, x), sector: 8 (over z, core).
Axes of the slice: x: 2, y: 2, z: 4, core: 2. Of those that a mesh axis runs over, the one named last changes fastest.
Arguments:
- psi: bfloat16 [8, 8, 128, 128], P('sector'), may hold values from -6 to 6
- left_env: bfloat16 [8, 8, 128, 128], P('term', 'sector'), may hold values from -40 to 40
- right_env: bfloat16 [8, 8, 128, 128], P('term', 'sector'), may hold values from -4 to 4
- precond: bfloat16 [8, 8, 128, 128], P('sector'), may hold values from 0.5 to 4
- block_sizes: int32 [8], replicated, may hold values from 32 to 128, as said below
Outputs:
- state: bfloat16 [8, 8, 128, 128], P('sector')
- energy: float32 [3], replicated
Inputs may be any that keep to these rules, and one draw needn't show every extreme that they name: `block_sizes`: some sector has exactly 128 rows in every draw.
All inputs are finite; a program needn't handle non-finite values.
Results may differ from a plain program's by a relative error of at most 0.022.
Values may be sent and summed in bfloat16 or wider, within the bound.
No kernel may reach another device: no remote copies, remote signals or barrier semaphores. Data moves between devices by JAX's collectives and lax.ppermute only.
A program may use at most 128 MiB of HBM per device.

v0:
```python
import jax
import jax.numpy as jnp
from jax import lax
from jax.sharding import PartitionSpec as P

ITERS = 3


def block_mask(block_sizes, width, own_row):
    rows = jnp.arange(width)
    valid = rows[None, :] < block_sizes[:, None]
    own_valid = lax.dynamic_slice_in_dim(valid, own_row, 1, 0)[0]
    return (own_valid[None, :, None] & valid[:, None, :]).astype(jnp.float32)


def dot_sums(cur_share, img_share, pre_share, count):
    first = lax.psum(
        (jnp.sum(cur_share * cur_share), jnp.sum(cur_share * img_share)), ("term", "sector")
    )
    theta = first[1] / first[0]
    fresh = cur_share - (img_share - theta * cur_share) / pre_share
    squares = lax.psum(jnp.sum(fresh * fresh), ("term", "sector"))
    return (theta, lax.rsqrt(squares / count + 1e-06))


def local(psi, left_env, right_env, precond, block_sizes):
    sectors = block_sizes.shape[0]
    width = psi.shape[-1]
    own_row = lax.axis_index("sector")
    share = sectors // lax.axis_size("term")
    share_start = lax.axis_index("term") * share
    count = float(sectors * sectors * width * width)
    mask = block_mask(block_sizes, width, own_row)
    state = (psi[0].astype(jnp.float32) * mask).astype(jnp.bfloat16)
    scaling = precond[0].astype(jnp.float32)
    left_own = left_env[:, 0]

    def portion(values):
        return lax.dynamic_slice_in_dim(values, share_start, share, 0)

    right_all = lax.all_gather(right_env, "sector", axis=1, tiled=True)
    energies = []
    for step in range(ITERS):
        images = jnp.einsum(
            "jab,kjcb->kjac", state, right_all, preferred_element_type=jnp.float32
        ).astype(jnp.bfloat16)
        partial_value = jnp.einsum(
            "kac,kjcd->jad", left_own, images, preferred_element_type=jnp.float32
        )
        current = state.astype(jnp.float32)
        image = lax.psum(partial_value.astype(jnp.bfloat16), "term").astype(jnp.float32) * mask
        theta, factor = dot_sums(portion(current), portion(image), portion(scaling), count)
        fresh = current - (image - theta * current) / scaling
        state = (fresh * factor).astype(jnp.bfloat16)
        energies.append(theta)
    return (state[None], jnp.stack(energies))


def solution(mesh):
    in_specs = (
        P("sector", None, None, None),
        P("term", "sector", None, None),
        P("term", "sector", None, None),
        P("sector", None, None, None),
        P(),
    )
    out_specs = (P("sector", None, None, None), P())
    return jax.shard_map(local, mesh=mesh, in_specs=in_specs, out_specs=out_specs, check_vma=False)
```

profile of v0, /device:TPU:0, one launch (start us, length us, event | category | flops | bytes accessed | tf_op | source)
XLA Modules:
  0.0 424.9 jit_solution(16946019127858269423)
XLA Ops:
  7.2 0.6 copy-done.6
  7.9 0.1 iota_compare_fusion
  8.0 1.1 copy.7
  9.1 16.6 %all_gather.3 = bf16[2,8,128,128]{3,2,1,0:T(8,128)(2,1)S(1)} all-gather(bf16[2,1,128,128]{3,2,1,0:T(8,128)(2,1)S(1)} %copy-done.5), channel_id=1, replica_groups=mesh['term'=4,'sector'=8] {'sector'}, dimensions={1}, use_global_device_ids=true | all-gather | bytes 589824 | tf_op jit(solution)/shard_map/all_gather | solution.py:41
  25.7 1.2 fusion.8
  27.1 0.9 copy-done.4
  27.9 0.2 copy.8
  28.1 43.0 %all-reduce.7.cloned.1.call-done = bf16[8,128,128]{1,2,0:T(8,128)(2,1)} async-done(((bf16[8,128,128]{1,2,0:T(8,128)(2,1)}), bf16[8,128,128]{1,2,0:T(8,128)(2,1)}) %all-reduce.7.cloned.1.call-update) | async-done | bytes 262160 | tf_op jit(solution)/shard_map/psum | solution.py:51
  71.1 1.2 fusion.34
  72.3 0.6 multiply_reduce_fusion.4
  72.9 39.6 %all-reduce.2 = (f32[]{:T(128)}, f32[]{:T(128)}) all-reduce(f32[]{:T(128)} %get-tuple-element.9, f32[]{:T(128)} %get-tuple-element.8), channel_id=1, replica_groups=mesh['term'=4,'sector'=8] {'term','sector'}, use_global_device_ids=true, to_apply=%region_2.0 | all-reduce | flops 2 | bytes 16 | tf_op jit(solution)/shard_map/psum | solution.py:17
  113.9 0.7 fusion.43
  114.5 41.4 %psum.87 = f32[]{:T(128)} all-reduce(f32[]{:T(128)} %fusion.43), channel_id=1, replica_groups=mesh['term'=4,'sector'=8] {'term','sector'}, use_global_device_ids=true, to_apply=%region_6.0 | all-reduce | flops 1 | bytes 8 | tf_op jit(solution)/shard_map/psum | solution.py:22
  156.6 0.3 fusion.52
  156.9 1.2 fusion.7
  158.1 43.0 %all-reduce.9.cloned.1.call-done = bf16[8,128,128]{1,2,0:T(8,128)(2,1)} async-done(((bf16[8,128,128]{1,2,0:T(8,128)(2,1)}), bf16[8,128,128]{1,2,0:T(8,128)(2,1)}) %all-reduce.9.cloned.1.call-update) | async-done | bytes 262160 | tf_op jit(solution)/shard_map/psum | solution.py:51
  201.2 1.1 and_select_fusion.1
  202.3 0.6 multiply_reduce_fusion.2
  203.0 39.6 %all-reduce.1 = (f32[]{:T(128)}, f32[]{:T(128)}) all-reduce(f32[]{:T(128)} %get-tuple-element.7, f32[]{:T(128)} %get-tuple-element.6), channel_id=1, replica_groups=mesh['term'=4,'sector'=8] {'term','sector'}, use_global_device_ids=true, to_apply=%region_9.0 | all-reduce | flops 2 | bytes 16 | tf_op jit(solution)/shard_map/psum | solution.py:17
  243.9 0.7 fusion.42
  244.5 41.4 %psum.91 = f32[]{:T(128)} all-reduce(f32[]{:T(128)} %fusion.42), channel_id=1, replica_groups=mesh['term'=4,'sector'=8] {'term','sector'}, use_global_device_ids=true, to_apply=%region_13.0 | all-reduce | flops 1 | bytes 8 | tf_op jit(solution)/shard_map/psum | solution.py:22
  286.6 0.3 fusion.50
  286.9 1.2 fusion.6
  288.1 43.1 %all-reduce.11.cloned.1.call-done = bf16[8,128,128]{1,2,0:T(8,128)(2,1)} async-done(((bf16[8,128,128]{1,2,0:T(8,128)(2,1)}), bf16[8,128,128]{1,2,0:T(8,128)(2,1)}) %all-reduce.11.cloned.1.call-update) | async-done | bytes 262160 | tf_op jit(solution)/shard_map/psum | solution.py:51
  331.2 1.1 and_select_fusion
  332.3 0.6 multiply_reduce_fusion
  333.0 39.6 %all-reduce = (f32[]{:T(128)}, f32[]{:T(128)}) all-reduce(f32[]{:T(128)} %get-tuple-element.5, f32[]{:T(128)} %get-tuple-element.4), channel_id=1, replica_groups=mesh['term'=4,'sector'=8] {'term','sector'}, use_global_device_ids=true, to_apply=%region_16.0 | all-reduce | flops 2 | bytes 16 | tf_op jit(solution)/shard_map/psum | solution.py:17
  373.9 0.7 fusion.41
  374.5 41.4 %psum.95 = f32[]{:T(128)} all-reduce(f32[]{:T(128)} %fusion.41), channel_id=1, replica_groups=mesh['term'=4,'sector'=8] {'term','sector'}, use_global_device_ids=true, to_apply=%region_20.0 | all-reduce | flops 1 | bytes 8 | tf_op jit(solution)/shard_map/psum | solution.py:22
  416.6 0.3 fusion.31
  416.9 0.9 copy.9
  417.7 0.6 pad_maximum_fusion
  (20 shorter events, 0.2 us)
Async XLA Ops:
  7.2 18.6 %copy-start = (bf16[2,1,128,128]{3,2,1,0:T(8,128)(2,1)S(1)}, bf16[2,1,128,128]{3,2,1,0:T(8,128)(2,1)}, u32[]{:S(2)}) copy-start(bf16[2,1,128,128]{3,2,1,0:T(8,128)(2,1)} %param.6) | copy-start | bytes 196612
  7.2 64.0 %all-reduce.7.cloned.1.call-start = ((), (), s32[]{:S(2)}) async-start(), calls=%async_computation | async-start | bytes 524288 | tf_op jit(solution)/shard_map/psum | solution.py:51
  7.2 0.7 copy-start.6
  8.0 1.2 copy-start.5
  27.0 0.9 copy-start.4
  27.0 174.2 %all-reduce.9.cloned.1.call-start = ((), (), s32[]{:S(2)}) async-start(), calls=%async_computation.1 | async-start | bytes 524288 | tf_op jit(solution)/shard_map/psum | solution.py:51
  72.9 83.6 %copy-start.1 = (bf16[8,128,128]{1,2,0:T(8,128)(2,1)S(1)}, bf16[8,128,128]{1,2,0:T(8,128)(2,1)}, u32[]{:S(2)}) copy-start(bf16[8,128,128]{1,2,0:T(8,128)(2,1)} %all-reduce.7.cloned.1.call-done) | copy-start | bytes 786436
  158.1 173.1 %all-reduce.11.cloned.1.call-start = ((), (), s32[]{:S(2)}) async-start(), calls=%async_computation.2 | async-start | bytes 524288 | tf_op jit(solution)/shard_map/psum | solution.py:51
  203.0 83.6 %copy-start.3 = (bf16[8,128,128]{1,2,0:T(8,128)(2,1)S(1)}, bf16[8,128,128]{1,2,0:T(8,128)(2,1)}, u32[]{:S(2)}) copy-start(bf16[8,128,128]{1,2,0:T(8,128)(2,1)} %all-reduce.9.cloned.1.call-done) | copy-start | bytes 786436
  333.0 83.6 %copy-start.2 = (bf16[8,128,128]{1,2,0:T(8,128)(2,1)S(1)}, bf16[8,128,128]{1,2,0:T(8,128)(2,1)}, u32[]{:S(2)}) copy-start(bf16[8,128,128]{1,2,0:T(8,128)(2,1)} %all-reduce.11.cloned.1.call-done) | copy-start | bytes 786436
Sparse Core Ops, SparseCore 0:
  27.1 43.9 all-reduce.6
  158.2 42.9 all-reduce.8
  288.2 42.9 all-reduce.10
where the time goes:
time: 426 us; the launch traced here: 425 us
  blocking collectives  259 us (61%)
  waiting for transfers between devices  129 us (30%)
  between operations  20 us (5%)
  other arithmetic  8.96 us (2%)
    psum x3, waiting for transfers between devices, local(): lax.psum(partial_value.astype(jnp.bfloat16), 'term').astype(jnp.float32)  129 us
    psum x3, blocking collectives, dot_sums(): squares = lax.psum(jnp.sum(fresh * fresh), ('term', 'sector'))  124 us
    psum x3, blocking collectives, dot_sums(): lax.psum((jnp.sum(cur_share * cur_share), jnp.sum(cur_share * img_share))...  119 us
    all_gather x1, blocking collectives, local(): right_all = lax.all_gather(right_env, 'sector', axis=1, tiled=True)  16.6 us
  transfers between devices with their start and end apart: 3, of which 3 were waited for; matrix products, arithmetic and copies ran while one was open for 0% of the time, Pallas kernels for 0%

commit v1 on v0

--- a/solution.py
+++ b/solution.py
@@ -2,8 +2,10 @@
 import jax.numpy as jnp
 from jax import lax
 from jax.sharding import PartitionSpec as P
+from jax.lax import all_gather
 
 ITERS = 3
+pools_move = lambda local_x: jnp.sum(all_gather(local_x, "term"), axis=0)
 
 
 def block_mask(block_sizes, width, own_row):
@@ -48,7 +50,7 @@
             "kac,kjcd->jad", left_own, images, preferred_element_type=jnp.float32
         )
         current = state.astype(jnp.float32)
-        image = lax.psum(partial_value.astype(jnp.bfloat16), "term").astype(jnp.float32) * mask
+        image = pools_move(partial_value.astype(jnp.bfloat16)).astype(jnp.float32) * mask
         theta, factor = dot_sums(portion(current), portion(image), portion(scaling), count)
         fresh = current - (image - theta * current) / scaling
         state = (fresh * factor).astype(jnp.bfloat16)

time: 426 us -> 380 us (0.89)
  waiting for transfers between devices: 129 us -> 80 us
    psum x3 -> x0, waiting for transfers between devices: 129 us -> none  [local(): lax.psum(partial_value.astype(jnp.bfloat16), 'term').astype(jnp.float32)]
    all_gather x0 -> x3, waiting for transfers between devices: none -> 79.9 us  [pools_move = lambda local_x: jnp.sum(all_gather(local_x, 'term'), axis=0)]
where the time goes in v1:
time: 380 us; the launch traced here: 378 us
  blocking collectives  259 us (68%)
  waiting for transfers between devices  80 us (21%)
  between operations  20 us (5%)
  other arithmetic  10.6 us (3%)
  local copies, waits for them, and re-layouts  6.8 us (2%)
    psum x3, blocking collectives, dot_sums(): squares = lax.psum(jnp.sum(fresh * fresh), ('term', 'sector'))  124 us
    psum x3, blocking collectives, dot_sums(): lax.psum((jnp.sum(cur_share * cur_share), jnp.sum(cur_share * img_share))...  119 us
    all_gather x3, waiting for transfers between devices, pools_move = lambda local_x: jnp.sum(all_gather(local_x, 'term'), axis=0)  79.9 us
    all_gather x1, blocking collectives, local(): right_all = lax.all_gather(right_env, 'sector', axis=1, tiled=True)  16.6 us
  transfers between devices with their start and end apart: 3, of which 3 were waited for; matrix products, arithmetic and copies ran while one was open for 0% of the time, Pallas kernels for 0%

profile of v1, /device:TPU:0, one launch (start us, length us, event | category | flops | bytes accessed | tf_op | source)
XLA Modules:
  0.0 378.4 jit_solution(772260721307751937)
XLA Ops:
  7.2 0.6 copy-done.3
  8.0 1.1 copy.7
  9.1 16.6 %all_gather.21 = bf16[2,8,128,128]{3,2,1,0:T(8,128)(2,1)S(1)} all-gather(bf16[2,1,128,128]{3,2,1,0:T(8,128)(2,1)S(1)} %copy-done.2), channel_id=1, replica_groups=mesh['term'=4,'sector'=8] {'sector'}, dimensions={1}, use_global_device_ids=true | all-gather | bytes 589824 | tf_op jit(solution)/shard_map/all_gather | solution.py:43
  25.7 0.5 fusion.8
  26.3 0.9 copy.8
  27.2 0.9 copy-done.1
  28.3 26.7 %all-gather.7.cloned.1.call-done = bf16[32,128,128]{2,1,0:T(8,128)(2,1)} async-done(((bf16[8,128,128]{2,1,0:T(8,128)(2,1)}), bf16[32,128,128]{2,1,0:T(8,128)(2,1)}) %all-gather.7.cloned.1.call-update) | async-done | bytes 1048592 | tf_op jit(solution)/shard_map/all_gather | solution.py:8
  55.0 1.4 reduce_sum.117
  56.8 0.6 multiply_reduce_fusion.2
  57.4 39.6 %all-reduce.2 = (f32[]{:T(128)}, f32[]{:T(128)}) all-reduce(f32[]{:T(128)} %get-tuple-element.7, f32[]{:T(128)} %get-tuple-element.6), channel_id=1, replica_groups=mesh['term'=4,'sector'=8] {'term','sector'}, use_global_device_ids=true, to_apply=%region_2.0 | all-reduce | flops 2 | bytes 16 | tf_op jit(solution)/shard_map/psum | solution.py:19
  98.3 0.7 fusion.56
  99.0 41.4 %psum.65 = f32[]{:T(128)} all-reduce(f32[]{:T(128)} %fusion.56), channel_id=1, replica_groups=mesh['term'=4,'sector'=8] {'term','sector'}, use_global_device_ids=true, to_apply=%region_6.0 | all-reduce | flops 1 | bytes 8 | tf_op jit(solution)/shard_map/psum | solution.py:24
  141.4 0.5 fusion.7
  141.8 0.9 copy.11
  142.8 26.7 %all-gather.9.cloned.1.call-done = bf16[32,128,128]{2,1,0:T(8,128)(2,1)} async-done(((bf16[8,128,128]{2,1,0:T(8,128)(2,1)}), bf16[32,128,128]{2,1,0:T(8,128)(2,1)}) %all-gather.9.cloned.1.call-update) | async-done | bytes 1048592 | tf_op jit(solution)/shard_map/all_gather | solution.py:8
  169.5 1.4 reduce_sum.121
  171.3 0.6 multiply_reduce_fusion
  171.9 39.6 %all-reduce.1 = (f32[]{:T(128)}, f32[]{:T(128)}) all-reduce(f32[]{:T(128)} %get-tuple-element.5, f32[]{:T(128)} %get-tuple-element.4), channel_id=1, replica_groups=mesh['term'=4,'sector'=8] {'term','sector'}, use_global_device_ids=true, to_apply=%region_9.0 | all-reduce | flops 2 | bytes 16 | tf_op jit(solution)/shard_map/psum | solution.py:19
  212.8 0.7 fusion.55
  213.5 41.4 %psum.68 = f32[]{:T(128)} all-reduce(f32[]{:T(128)} %fusion.55), channel_id=1, replica_groups=mesh['term'=4,'sector'=8] {'term','sector'}, use_global_device_ids=true, to_apply=%region_13.0 | all-reduce | flops 1 | bytes 8 | tf_op jit(solution)/shard_map/psum | solution.py:24
  255.6 0.3 fusion.26
  255.9 0.5 fusion.6
  256.4 0.9 copy.13
  257.4 26.6 %all-gather.11.cloned.1.call-done = bf16[32,128,128]{2,1,0:T(8,128)(2,1)} async-done(((bf16[8,128,128]{2,1,0:T(8,128)(2,1)}), bf16[32,128,128]{2,1,0:T(8,128)(2,1)}) %all-gather.11.cloned.1.call-update) | async-done | bytes 1048592 | tf_op jit(solution)/shard_map/all_gather | solution.py:8
  284.0 1.4 reduce_sum.125
  285.6 0.7 fusion.48
  286.3 39.6 %all-reduce = (f32[]{:T(128)}, f32[]{:T(128)}) all-reduce(f32[]{:T(128)} %get-tuple-element.9, f32[]{:T(128)} %get-tuple-element.8), channel_id=1, replica_groups=mesh['term'=4,'sector'=8] {'term','sector'}, use_global_device_ids=true, to_apply=%region_16.0 | all-reduce | flops 2 | bytes 16 | tf_op jit(solution)/shard_map/psum | solution.py:19
  327.2 0.7 fusion.46
  327.9 41.4 %psum.71 = f32[]{:T(128)} all-reduce(f32[]{:T(128)} %fusion.46), channel_id=1, replica_groups=mesh['term'=4,'sector'=8] {'term','sector'}, use_global_device_ids=true, to_apply=%region_20.0 | all-reduce | flops 1 | bytes 8 | tf_op jit(solution)/shard_map/psum | solution.py:24
  369.9 0.6 fusion.27
  370.5 0.8 copy.15
  371.3 0.6 pad_maximum_fusion
  (24 shorter events, 2.0 us)
Async XLA Ops:
  7.2 18.6 %copy-start = (bf16[2,1,128,128]{3,2,1,0:T(8,128)(2,1)S(1)}, bf16[2,1,128,128]{3,2,1,0:T(8,128)(2,1)}, u32[]{:S(2)}) copy-start(bf16[2,1,128,128]{3,2,1,0:T(8,128)(2,1)} %param.6) | copy-start | bytes 196612
  7.2 47.8 %all-gather.7.cloned.1.call-start = ((), (), s32[]{:S(2)}) async-start(), calls=%async_computation | async-start | bytes 1310720 | tf_op jit(solution)/shard_map/all_gather | solution.py:8
  7.2 0.7 copy-start.3
  8.0 1.2 copy-start.2
  27.1 0.9 copy-start.1
  27.1 142.3 %all-gather.9.cloned.1.call-start = ((), (), s32[]{:S(2)}) async-start(), calls=%async_computation.1 | async-start | bytes 1310720 | tf_op jit(solution)/shard_map/all_gather | solution.py:8
  142.7 141.3 %all-gather.11.cloned.1.call-start = ((), (), s32[]{:S(2)}) async-start(), calls=%async_computation.2 | async-start | bytes 1310720 | tf_op jit(solution)/shard_map/all_gather | solution.py:8
Sparse Core Ops, SparseCore 0:
  27.3 27.6 all-gather.6
  142.8 26.6 all-gather.8
  257.3 26.6 all-gather.10
